TPU v7x, 32 devices: a whole 2x2x4 slice. The times are simulated.
32 devices in a mesh: chan: 4 (over y, core), blk: 8 (over z, x).
Axes of the slice: x: 2, y: 2, z: 4, core: 2. Of those that a mesh axis runs over, the one named last changes fastest.
Arguments:
- comp_alms: float32 [3, 4, 8, 4096], P(None, None, 'blk', 'chan'), may hold values from -6 to 6
- legendre: bfloat16 [2, 8, 4096, 32], P(None, 'blk'), may hold values from -0.09375 to 0.09375
- inv_noise: float32 [4, 2, 32, 8192], P('chan', None, 'blk'), may hold values from 0.5 to 5
- beam_window: float32 [4, 4096], replicated, may hold values from 0.1 to 1
- mixing: float32 [4, 3], replicated, may hold values from 0.2 to 1.5
- channel_of: int32 [4], replicated, may hold values from 0 to 3, each once
- m_orders: int32 [8], replicated, may hold values from 0 to 4095, as said below
- cycle_of: int32 [32], replicated, may hold values from 0 to 31, each once
- cycle_pixels: int32 [32], replicated, may hold values from 4 to 8192, as said below
Outputs:
- normal_product: float32 [3, 4, 8, 4096], P(None, None, 'blk', 'chan')
Inputs may be any that keep to these rules, and one draw needn't show every extreme that they name: `m_orders`: the orders are distinct. `cycle_pixels`: each entry is 4 * min(h, 2048, 8192 - h) for some cycle number h of 1 to 8191; at least one entry equals 8192.
All inputs are finite; a program needn't handle non-finite values.
Results may differ from a plain program's by a relative error of at most 0.0022.
Values may be sent and summed in bfloat16 or wider, within the bound.
A program may use at most 128 MiB of HBM per device.

v0:
```python
import math
import jax
import jax.numpy as jnp
from jax import lax
from jax.sharding import PartitionSpec as P


def phase_rows(orders, pix_count, cycle_width):
    columns = jnp.arange(cycle_width, dtype=jnp.int32)
    phase_steps = orders[:, None] * (2 * columns[None, :] + 1) % (2 * pix_count)
    angles = phase_steps.astype(jnp.float32) * (
        jnp.float32(math.pi) / pix_count.astype(jnp.float32)
    )
    return jnp.concatenate([jnp.cos(angles), jnp.sin(angles)], axis=0).astype(jnp.bfloat16)


def combine_forward(plus_sum, minus_sum):
    return jnp.stack(
        [
            plus_sum[:, 0] - minus_sum[:, 3],
            plus_sum[:, 1] + minus_sum[:, 2],
            plus_sum[:, 2] + minus_sum[:, 1],
            plus_sum[:, 3] - minus_sum[:, 0],
        ],
        axis=1,
    )


def twist_grads(cycle_grads):
    return jnp.stack(
        [-cycle_grads[:, 3], cycle_grads[:, 2], cycle_grads[:, 1], -cycle_grads[:, 0]], axis=1
    )


def cycle_work(coeffs, weights, orders, pix_count):
    slots = coeffs.shape[0]
    cycle_width = weights.shape[-1]
    phases = phase_rows(orders, pix_count, cycle_width)
    half_rows = phases.shape[0] // 2
    real_part = coeffs[:, 0::2]
    imag_part = coeffs[:, 1::2]
    stacked = jnp.concatenate([real_part, -imag_part], axis=2).reshape(2 * slots, 2 * half_rows)
    maps = jnp.dot(stacked, phases, preferred_element_type=jnp.float32)
    live_mask = jnp.arange(cycle_width, dtype=jnp.int32) < pix_count
    scaled = jnp.where(live_mask[None, None, :], weights, 0.0) / pix_count.astype(jnp.float32)
    weighted = (scaled.reshape(maps.shape) * maps).astype(jnp.bfloat16)
    returned = lax.dot_general(
        weighted, phases, (((1,), (1,)), ((), ())), preferred_element_type=jnp.float32
    )
    grad_real = returned[:, :half_rows].reshape(slots, 2, half_rows)
    grad_imag = (-returned[:, half_rows:]).reshape(slots, 2, half_rows)
    return (
        jnp.stack([grad_real, grad_imag], axis=2).reshape(slots, 4, half_rows).astype(jnp.bfloat16)
    )


def mix_components(mix_rows, components):
    accum = mix_rows[:, 0, None, None, None] * components[0][None]
    for comp_index in range(1, components.shape[0]):
        accum = accum + mix_rows[:, comp_index, None, None, None] * components[comp_index][None]
    return accum


def body(
    comp_alms,
    legendre,
    inv_noise,
    beam_window,
    mixing,
    channel_of,
    m_orders,
    cycle_of,
    cycle_pixels,
):
    chan_index = lax.axis_index("chan")
    blk_index = lax.axis_index("blk")
    order_dev = comp_alms.shape[2]
    shard_len = comp_alms.shape[3]
    length = legendre.shape[2]
    cycle_total = legendre.shape[3]
    chan_dev = inv_noise.shape[0]
    cycle_dev = inv_noise.shape[2]
    block_len = min(512, length)
    blocks = length // block_len
    own_orders = lax.dynamic_slice_in_dim(m_orders, blk_index * order_dev, order_dev)
    keep_mask = (jnp.arange(length, dtype=jnp.int32)[None, :] >= own_orders[:, None]).astype(
        jnp.float32
    )
    picked = lax.dynamic_slice_in_dim(channel_of, chan_index * chan_dev, chan_dev)
    mix_rows = jnp.take(mixing, picked, axis=0)
    beam_rows = jnp.take(beam_window, picked, axis=0)
    mix_all = jnp.take(mixing, channel_of, axis=0)
    beam_piece = jnp.take(
        lax.dynamic_slice_in_dim(beam_window, chan_index * shard_len, shard_len, 1),
        channel_of,
        axis=0,
    )
    gathered = lax.all_gather(comp_alms, "chan", axis=3, tiled=True)
    mixed_alm = mix_components(mix_rows, gathered)
    chan_alm = (mixed_alm * beam_rows[:, None, None, :] * keep_mask[None, None]).astype(
        jnp.bfloat16
    )
    order = 0
    row_block = chan_alm[:, :, order, :].reshape(chan_dev * 4, length)
    first_block = own_orders[order] // block_len

    def add_block(index, running, row_block=row_block, order=order):
        plus_sum, minus_sum = running
        offset = index * block_len
        segment = lax.dynamic_slice_in_dim(row_block, offset, block_len, 1)
        tables = lax.dynamic_slice(legendre, (0, order, offset, 0), (2, 1, block_len, cycle_total))
        plus_sum = plus_sum + jnp.dot(segment, tables[0, 0], preferred_element_type=jnp.float32)
        minus_sum = minus_sum + jnp.dot(segment, tables[1, 0], preferred_element_type=jnp.float32)
        return (plus_sum, minus_sum)

    zeros_cycle = jnp.zeros((chan_dev * 4, cycle_total), jnp.float32)
    plus_sum, minus_sum = lax.fori_loop(first_block, blocks, add_block, (zeros_cycle, zeros_cycle))
    coeff_list = [
        combine_forward(
            plus_sum.reshape(chan_dev, 4, cycle_total), minus_sum.reshape(chan_dev, 4, cycle_total)
        )
    ]
    cycle_coeffs = jnp.stack(coeff_list, axis=2).astype(jnp.bfloat16)
    slot_coeffs = jnp.take(cycle_coeffs, cycle_of, axis=3)
    by_cycle = lax.all_to_all(slot_coeffs, "blk", split_axis=3, concat_axis=2, tiled=True)
    first_slot = blk_index * cycle_dev

    def per_cycle(index, collected):
        coeffs = lax.dynamic_index_in_dim(by_cycle, index, 3, keepdims=False)
        weights = lax.dynamic_index_in_dim(inv_noise, index, 2, keepdims=False)
        pix_count = cycle_pixels[cycle_of[first_slot + index]]
        result = cycle_work(coeffs, weights, m_orders, pix_count)
        return lax.dynamic_update_index_in_dim(collected, result, index, 3)

    slot_grads = lax.fori_loop(0, cycle_dev, per_cycle, jnp.zeros(by_cycle.shape, jnp.bfloat16))
    returned = lax.all_to_all(slot_grads, "blk", split_axis=2, concat_axis=3, tiled=True)
    inverse = (
        jnp.zeros((cycle_total,), jnp.int32)
        .at[cycle_of]
        .set(jnp.arange(cycle_total, dtype=jnp.int32))
    )
    cycle_grads = jnp.take(returned, inverse, axis=3)
    order = 0
    order_grads = cycle_grads[:, :, order, :]
    twisted = twist_grads(order_grads).reshape(chan_dev * 4, cycle_total)
    straight = order_grads.reshape(chan_dev * 4, cycle_total)
    first_block = own_orders[order] // block_len

    def add_degrees(index, accum, straight=straight, twisted=twisted, order=order):
        offset = index * block_len
        tables = lax.dynamic_slice(legendre, (0, order, offset, 0), (2, 1, block_len, cycle_total))
        segment = lax.dot_general(
            straight, tables[0, 0], (((1,), (1,)), ((), ())), preferred_element_type=jnp.float32
        )
        segment = segment + lax.dot_general(
            twisted, tables[1, 0], (((1,), (1,)), ((), ())), preferred_element_type=jnp.float32
        )
        return lax.dynamic_update_slice_in_dim(accum, segment, offset, 1)

    accum = lax.fori_loop(
        first_block, blocks, add_degrees, jnp.zeros((chan_dev * 4, length), jnp.float32)
    )
    grad_list = [accum.reshape(chan_dev, 4, length)]
    alm_grads = jnp.stack(grad_list, axis=2) * keep_mask[None, None]
    received = lax.all_to_all(alm_grads, "chan", split_axis=3, concat_axis=0, tiled=True)
    beamed = received * beam_piece[:, None, None, :]
    return jnp.einsum("kc,kpml->cpml", mix_all, beamed, precision=lax.Precision.HIGHEST)


def solution(mesh):
    in_specs = (
        P(None, None, "blk", "chan"),
        P(None, "blk", None, None),
        P("chan", None, "blk", None),
        P(),
        P(),
        P(),
        P(),
        P(),
        P(),
    )
    out_specs = P(None, None, "blk", "chan")
    return jax.shard_map(body, mesh=mesh, in_specs=in_specs, out_specs=out_specs, check_vma=False)
```

profile of v0, /device:TPU:8, one launch (start us, length us, event | category | flops | bytes accessed | tf_op | source)
XLA Modules:
  0.0 151.8 jit_solution(12657113365354323406)
XLA Ops:
  5.2 1.3 dynamic_slice.49
  11.4 5.6 %all_gather.3 = f32[3,4,1,4096]{3,1,2,0:T(4,128)S(1)} all-gather(f32[3,4,1,1024]{3,1,2,0:T(4,128)S(1)} %copy.31), channel_id=1, replica_groups=mesh['chan'=4,'blk'=8] {'chan'}, dimensions={3}, use_global_device_ids=true | all-gather | bytes 245760 | tf_op jit(solution)/shard_map/all_gather | solution.py:98
  17.6 1.9 %fusion.43 = bf16[4,4096]{1,0:T(4,128)(2,1)S(1)} fusion(f32[4096]{0:T(1024)S(1)} %fusion.44, f32[4096]{0:T(1024)S(1)} %bitcast.126, f32[3,4,1,4096]{3,1,2,0:T(4,128)S(1)} %all_gather.3, f32[]{:T(128)} %bitcast.19, f32[]{:T(128)} %bitcast.18, f32[]{:T(128)} %bitcast.17), kind=kLoop, calls=%fused_computation.70 | loop fusion | flops 131072 | bytes 262156 | tf_op jit(solution)/shard_map/reshape;squeeze | solution.py:104
  19.6 8.9 %while.37 = (s32[]{:T(128)}, f32[4,32]{1,0:T(4,128)S(1)}, f32[4,32]{1,0:T(4,128)S(1)}, bf16[4,4096]{1,0:T(4,128)(2,1)S(1)}, bf16[2,1,4096,32]{2,3,1,0:T(8,128)(2...) while((s32[]{:T(128)}, f32[4,32]{1,0:T(4,128)S(1)}, f32[4,32]{1,0:T(4,128)S(1)}, ...), condition=%wide.region_1.2_spmd, body=%wide.region_0.1_spmd.sunk | while | flops 262407 | bytes 81567 | solution.py:117
  30.0 5.3 %all-to-all-start = ((bf16[1,4,1,32]{1,2,0,3:T(2,128)(2,1)}), bf16[1,4,1,32]{1,2,0,3:T(2,128)(2,1)S(1)}, u32[]{:S(2)}, u32[]{:S(2)}) async-start(bf16[1,4,1,32]{1,2,0,3:T(2,128)(2,1)} %copy.34), calls=%async_computation | async-start | bytes 32768 | tf_op jit(solution)/shard_map/all_to_all | solution.py:125
  38.1 2.3 %all-to-all-done = bf16[1,4,1,32]{1,2,0,3:T(2,128)(2,1)S(1)} async-done(((bf16[1,4,1,32]{1,2,0,3:T(2,128)(2,1)}), bf16[1,4,1,32]{1,2,0,3:T(2,128)(2,1)S(1)}, u32[]{:S(2)}, u32[]{:S(2)}) %all-to-all-start) | async-done | bytes 288 | tf_op jit(solution)/shard_map/all_to_all | solution.py:125
  40.5 50.0 %while.38 = (s32[]{:T(128)}, bf16[1,4,8,4]{2,1,3,0:T(4,128)(2,1)S(1)}, s32[]{:T(128)}, s32[32]{0:T(128)}, s32[32]{0:T(128)}, /*index=5*/f32[1,2,4,8192]{3,2,1,0:...) while((s32[]{:T(128)}, ...), condition=%wide.region_3.5_spmd, body=%wide.region_2.4_spmd.sunk | while | flops 2973951 | bytes 806209 | solution.py:135
  46.3 4.4 %cosine_convert_fusion.2 = (bf16[8,8192]{1,0:T(8,128)(2,1)S(1)}, bf16[8,8192]{1,0:T(8,128)(2,1)S(1)}) fusion(f32[]{:T(128)S(6)} %div.51, s32[]{:T(128)S(6)} %select_n.210, s32[8192]{0:T(1024)S(1)} %multiply_add_fusion.2, s32[8]{0:T(128)} %get-tuple-element.485, pred[]{:T(512)S(6)} %lt.154), kind=kLoop, calls=%fused_computation.23.clone.1 | loop fusion | flops 786432 | bytes 294953 | tf_op jit(solution)/shard_map/convert.5
  53.0 1.2 dynamic_slice.68
  58.8 4.4 %cosine_convert_fusion.2 = (bf16[8,8192]{1,0:T(8,128)(2,1)S(1)}, bf16[8,8192]{1,0:T(8,128)(2,1)S(1)}) fusion(f32[]{:T(128)S(6)} %div.51, s32[]{:T(128)S(6)} %select_n.210, s32[8192]{0:T(1024)S(1)} %multiply_add_fusion.2, s32[8]{0:T(128)} %get-tuple-element.485, pred[]{:T(512)S(6)} %lt.154), kind=kLoop, calls=%fused_computation.23.clone.1 | loop fusion | flops 786432 | bytes 294953 | tf_op jit(solution)/shard_map/convert.5
  65.5 1.2 dynamic_slice.68
  71.3 4.4 %cosine_convert_fusion.2 = (bf16[8,8192]{1,0:T(8,128)(2,1)S(1)}, bf16[8,8192]{1,0:T(8,128)(2,1)S(1)}) fusion(f32[]{:T(128)S(6)} %div.51, s32[]{:T(128)S(6)} %select_n.210, s32[8192]{0:T(1024)S(1)} %multiply_add_fusion.2, s32[8]{0:T(128)} %get-tuple-element.485, pred[]{:T(512)S(6)} %lt.154), kind=kLoop, calls=%fused_computation.23.clone.1 | loop fusion | flops 786432 | bytes 294953 | tf_op jit(solution)/shard_map/convert.5
  78.0 1.2 dynamic_slice.68
  83.8 4.4 %cosine_convert_fusion.2 = (bf16[8,8192]{1,0:T(8,128)(2,1)S(1)}, bf16[8,8192]{1,0:T(8,128)(2,1)S(1)}) fusion(f32[]{:T(128)S(6)} %div.51, s32[]{:T(128)S(6)} %select_n.210, s32[8192]{0:T(1024)S(1)} %multiply_add_fusion.2, s32[8]{0:T(128)} %get-tuple-element.485, pred[]{:T(512)S(6)} %lt.154), kind=kLoop, calls=%fused_computation.23.clone.1 | loop fusion | flops 786432 | bytes 294953 | tf_op jit(solution)/shard_map/convert.5
  91.2 4.8 %all-to-all-start.1 = ((bf16[1,4,8,4]{1,3,0,2:T(4,128)(2,1)}), bf16[1,4,8,4]{1,3,0,2:T(4,128)(2,1)S(1)}, u32[]{:S(2)}, u32[]{:S(2)}) async-start(bf16[1,4,8,4]{1,3,0,2:T(4,128)(2,1)} %copy.38), calls=%async_computation.1 | async-start | bytes 16384 | tf_op jit(solution)/shard_map/all_to_all | solution.py:136
  96.6 4.5 %all-to-all-done.1 = bf16[1,4,8,4]{1,3,0,2:T(4,128)(2,1)S(1)} async-done(((bf16[1,4,8,4]{1,3,0,2:T(4,128)(2,1)}), bf16[1,4,8,4]{1,3,0,2:T(4,128)(2,1)S(1)}, u32[]{:S(2)}, u32[]{:S(2)}) %all-to-all-start.1) | async-done | bytes 288 | tf_op jit(solution)/shard_map/all_to_all | solution.py:136
  101.8 8.8 %while.39 = (s32[]{:T(128)}, f32[4,4096]{1,0:T(4,128)S(1)}, bf16[2,1,4096,32]{2,3,1,0:T(8,128)(2,1)}, bf16[4,32]{1,0:T(4,128)(2,1)S(1)}, bf16[4,32]{1,0:T(4,128)...) while((s32[]{:T(128)}, f32[4,4096]{1,0:T(4,128)S(1)}, ...), condition=%wide.region_6.8_spmd, body=%wide.region_5.7_spmd.sunk | while | flops 264199 | bytes 93091 | solution.py:160
  110.6 2.0 %copy.42 = f32[4,4096]{0,1:T(8,128)} copy(f32[4,4096]{1,0:T(4,128)S(1)} %get-tuple-element.203) | data formatting | bytes 131072 | tf_op jit(solution)/shard_map/while | solution.py:160
  112.6 2.2 %broadcast_multiply_fusion = f32[4,4096]{0,1:T(8,128)S(1)} fusion(f32[4,4096]{0,1:T(8,128)} %copy.42, f32[4096]{0:T(1024)S(1)} %fusion.44), kind=kLoop, calls=%fused_computation.58 | loop fusion | flops 16384 | bytes 147456 | tf_op jit(solution)/shard_map/mul | solution.py:164
  115.3 19.4 %reduce = f32[4096,4]{1,0:T(8,128)} reduce(f32[4096,1,1,4]{3,2,1,0:T(1,128)S(1)} %bitcast.121, f32[]{:T(128)} %broadcast.233), dimensions={1,2}, to_apply=%bitcast.83.reduce_sub_computation | reduce | bytes 131076
  134.7 3.9 %reshape.357 = f32[4,1,4096]{2,1,0:T(1,128)} reshape(f32[4096,4]{1,0:T(8,128)} %reduce) | data formatting | bytes 131072
  138.6 3.5 %all-to-all-start.2 = ((f32[4,1,4096]{2,1,0:T(1,128)}), f32[4,1,4096]{2,1,0:T(1,128)S(1)}, u32[]{:S(2)}, u32[]{:S(2)}) async-start(f32[4,1,4096]{2,1,0:T(1,128)} %reshape.357), calls=%async_computation.2 | async-start | bytes 131072 | tf_op jit(solution)/shard_map/all_to_all | solution.py:165
  142.7 3.3 %all-to-all-done.2 = f32[4,1,4096]{2,1,0:T(1,128)S(1)} async-done(((f32[4,1,4096]{2,1,0:T(1,128)}), f32[4,1,4096]{2,1,0:T(1,128)S(1)}, u32[]{:S(2)}, u32[]{:S(2)}) %all-to-all-start.2) | async-done | bytes 65568 | tf_op jit(solution)/shard_map/all_to_all | solution.py:165
  146.8 3.3 %reshape.358 = f32[4096,1,1,4]{3,2,1,0:T(1,128)S(1)} reshape(f32[4,4096]{1,0:T(4,128)S(1)} %reduce.1) | data formatting | bytes 131072
  (124 shorter events, 49.3 us)
Async XLA Ops:
  30.0 10.4 %all-to-all-start = ((bf16[1,4,1,32]{1,2,0,3:T(2,128)(2,1)}), bf16[1,4,1,32]{1,2,0,3:T(2,128)(2,1)S(1)}, u32[]{:S(2)}, u32[]{:S(2)}) async-start(bf16[1,4,1,32]{1,2,0,3:T(2,128)(2,1)} %copy.34), calls=%async_computation | async-start | bytes 32768 | tf_op jit(solution)/shard_map/all_to_all | solution.py:125
  91.2 9.8 %all-to-all-start.1 = ((bf16[1,4,8,4]{1,3,0,2:T(4,128)(2,1)}), bf16[1,4,8,4]{1,3,0,2:T(4,128)(2,1)S(1)}, u32[]{:S(2)}, u32[]{:S(2)}) async-start(bf16[1,4,8,4]{1,3,0,2:T(4,128)(2,1)} %copy.38), calls=%async_computation.1 | async-start | bytes 16384 | tf_op jit(solution)/shard_map/all_to_all | solution.py:136
  134.7 7.5 %copy-start = (f32[4,3]{1,0:T(4,128)S(1)}, f32[4,3]{1,0:T(4,128)}, u32[]{:S(2)}) copy-start(f32[4,3]{1,0:T(4,128)} %param.21) | copy-start | bytes 148
  138.6 7.4 %all-to-all-start.2 = ((f32[4,1,4096]{2,1,0:T(1,128)}), f32[4,1,4096]{2,1,0:T(1,128)S(1)}, u32[]{:S(2)}, u32[]{:S(2)}) async-start(f32[4,1,4096]{2,1,0:T(1,128)} %reshape.357), calls=%async_computation.2 | async-start | bytes 131072 | tf_op jit(solution)/shard_map/all_to_all | solution.py:165
where the time goes:
time: 154 us; the launch traced here: 152 us
  other arithmetic  49.9 us (32%)
  local copies, waits for them, and re-layouts  34.9 us (23%)
  matrix products  19.7 us (13%)
  starting transfers between devices  13.6 us (9%)
  loops' own time  13.5 us (9%)
  waiting for transfers between devices  10 us (6%)
  blocking collectives  5.6 us (4%)
  between operations  4.67 us (3%)
    unnamed x1, other arithmetic  19.4 us
    another operation x5, other arithmetic  17.5 us
    another operation x1, loops' own time, body(): lax.fori_loop(0, cycle_dev, per_cycle, jnp.zeros(by_cycle.shape, jnp.bflo...  13.4 us
    dynamic_slice x8, local copies, waits for them, and re-layouts, per_cycle(): pix_count = cycle_pixels[cycle_of[first_slot + index]]  9.93 us
    unnamed x7, local copies, waits for them, and re-layouts  8.55 us
    all_gather x1, blocking collectives, body(): gathered = lax.all_gather(comp_alms, 'chan', axis=3, tiled=True)  5.6 us
    all_to_all x1, starting transfers between devices, body(): lax.all_to_all(slot_coeffs, 'blk', split_axis=3, concat_axis=2, tiled=True)  5.32 us
    all_to_all x1, starting transfers between devices, body(): lax.all_to_all(slot_grads, 'blk', split_axis=2, concat_axis=3, tiled=True)  4.79 us
  transfers between devices with their start and end apart: 3, of which 3 were waited for; matrix products, arithmetic and copies ran while one was open for 3% of the time, Pallas kernels for 0%

commit v1 on v0

--- a/solution.py
+++ b/solution.py
@@ -3,6 +3,29 @@
 import jax.numpy as jnp
 from jax import lax
 from jax.sharding import PartitionSpec as P
+
+
+def in_blocks(x, dim, size):
+    lengths = x.shape
+    blocks = x.reshape(*lengths[:dim], size, lengths[dim] // size, *lengths[dim + 1 :])
+    return jnp.moveaxis(blocks, dim, 0)
+
+
+def in_order(blocks, dim):
+    dims = list(blocks.shape[1:])
+    dims[dim] *= blocks.shape[0]
+    return jnp.moveaxis(blocks, 0, dim).reshape(dims)
+
+
+def rotated_exchange(x, axis, split_dim, concat_dim):
+    peers, index = (lax.axis_size(axis), lax.axis_index(axis))
+    blocks = in_blocks(x, split_dim, peers)
+    gathered = [blocks[index]]
+    for turn in range(1, peers):
+        sent = blocks[(index + turn) % peers]
+        gathered.append(lax.ppermute(sent, axis, [(i, (i + turn) % peers) for i in range(peers)]))
+    blocks = jnp.stack(gathered)[(index - jnp.arange(peers)) % peers]
+    return in_order(blocks, concat_dim)
 
 
 def phase_rows(orders, pix_count, cycle_width):
@@ -133,7 +156,7 @@
         return lax.dynamic_update_index_in_dim(collected, result, index, 3)
 
     slot_grads = lax.fori_loop(0, cycle_dev, per_cycle, jnp.zeros(by_cycle.shape, jnp.bfloat16))
-    returned = lax.all_to_all(slot_grads, "blk", split_axis=2, concat_axis=3, tiled=True)
+    returned = rotated_exchange(slot_grads, "blk", 2, 3)
     inverse = (
         jnp.zeros((cycle_total,), jnp.int32)
         .at[cycle_of]

time: 154 us -> 158 us (1.026)
  starting transfers between devices: 13.6 us -> 19.6 us
  waiting for transfers between devices: 10 us -> 6.38 us
    ppermute x0 -> x7, starting transfers between devices: none -> 10.8 us  [rotated_exchange(): lax.ppermute(sent, axis, [(i, (i + turn) % peers) for i in range(peers)])]
    all_to_all x1 -> x0, starting transfers between devices: 4.79 us -> none  [body(): lax.all_to_all(slot_grads, 'blk', split_axis=2, concat_axis=3, tiled=True)]
    all_to_all x1 -> x0, waiting for transfers between devices: 4.48 us -> none  [body(): lax.all_to_all(slot_grads, 'blk', split_axis=2, concat_axis=3, tiled=True)]
    unnamed x7 -> x14, local copies, waits for them, and re-layouts: 8.55 us -> 8.61 us
  transfers between devices with their start and end apart: 3 -> 9, of which waited for: 3 -> 4; matrix products, arithmetic and copies ran while one was open for 3% -> 3% of each run, Pallas kernels for 0% -> 0%
where the time goes in v1:
time: 158 us; the launch traced here: 156 us
  other arithmetic  49.9 us (32%)
  local copies, waits for them, and re-layouts  36.2 us (23%)
  matrix products  19.7 us (12%)
  starting transfers between devices  19.6 us (12%)
  loops' own time  13.5 us (9%)
  waiting for transfers between devices  6.38 us (4%)
  blocking collectives  5.6 us (4%)
  between operations  4.91 us (3%)
    unnamed x1, other arithmetic  19.4 us
    another operation x5, other arithmetic  17.5 us
    another operation x1, loops' own time, body(): lax.fori_loop(0, cycle_dev, per_cycle, jnp.zeros(by_cycle.shape, jnp.bflo...  13.4 us
    ppermute x7, starting transfers between devices, rotated_exchange(): lax.ppermute(sent, axis, [(i, (i + turn) % peers) for i in range(peers)])  10.8 us
    dynamic_slice x8, local copies, waits for them, and re-layouts, per_cycle(): pix_count = cycle_pixels[cycle_of[first_slot + index]]  9.93 us
    unnamed x14, local copies, waits for them, and re-layouts  8.61 us
    all_gather x1, blocking collectives, body(): gathered = lax.all_gather(comp_alms, 'chan', axis=3, tiled=True)  5.6 us
    all_to_all x1, starting transfers between devices, body(): lax.all_to_all(slot_coeffs, 'blk', split_axis=3, concat_axis=2, tiled=True)  5.32 us
  transfers between devices with their start and end apart: 9, of which 4 were waited for; matrix products, arithmetic and copies ran while one was open for 3% of the time, Pallas kernels for 0%

profile of v1, /device:TPU:8, one launch (start us, length us, event | category | flops | bytes accessed | tf_op | source)
XLA Modules:
  0.0 155.7 jit_solution(13076562199894040492)
XLA Ops:
  5.2 1.3 dynamic_slice.59
  11.6 5.6 %all_gather.3 = f32[3,4,1,4096]{3,1,2,0:T(4,128)S(1)} all-gather(f32[3,4,1,1024]{3,1,2,0:T(4,128)S(1)} %copy.51), channel_id=1, replica_groups=mesh['chan'=4,'blk'=8] {'chan'}, dimensions={3}, use_global_device_ids=true | all-gather | bytes 245760 | tf_op jit(solution)/shard_map/all_gather | solution.py:121
  17.9 1.9 %fusion.43 = bf16[4,4096]{1,0:T(4,128)(2,1)S(1)} fusion(f32[4096]{0:T(1024)S(1)} %fusion.44, f32[4096]{0:T(1024)S(1)} %bitcast.146, f32[3,4,1,4096]{3,1,2,0:T(4,128)S(1)} %all_gather.3, f32[]{:T(128)} %bitcast.19, f32[]{:T(128)} %bitcast.18, f32[]{:T(128)} %bitcast.17), kind=kLoop, calls=%fused_computation.71 | loop fusion | flops 131072 | bytes 262156 | tf_op jit(solution)/shard_map/reshape;squeeze | solution.py:127
  19.8 8.9 %while.37 = (s32[]{:T(128)}, f32[4,32]{1,0:T(4,128)S(1)}, f32[4,32]{1,0:T(4,128)S(1)}, bf16[4,4096]{1,0:T(4,128)(2,1)S(1)}, bf16[2,1,4096,32]{2,3,1,0:T(8,128)(2...) while((s32[]{:T(128)}, f32[4,32]{1,0:T(4,128)S(1)}, f32[4,32]{1,0:T(4,128)S(1)}, ...), condition=%wide.region_1.2_spmd, body=%wide.region_0.1_spmd.sunk | while | flops 262407 | bytes 81567 | solution.py:140
  30.3 5.3 %all-to-all-start = ((bf16[1,4,1,32]{1,2,0,3:T(2,128)(2,1)}), bf16[1,4,1,32]{1,2,0,3:T(2,128)(2,1)S(1)}, u32[]{:S(2)}, u32[]{:S(2)}) async-start(bf16[1,4,1,32]{1,2,0,3:T(2,128)(2,1)} %copy.54), calls=%async_computation | async-start | bytes 32768 | tf_op jit(solution)/shard_map/all_to_all | solution.py:148
  39.0 1.6 %all-to-all-done = bf16[1,4,1,32]{1,2,0,3:T(2,128)(2,1)S(1)} async-done(((bf16[1,4,1,32]{1,2,0,3:T(2,128)(2,1)}), bf16[1,4,1,32]{1,2,0,3:T(2,128)(2,1)S(1)}, u32[]{:S(2)}, u32[]{:S(2)}) %all-to-all-start) | async-done | bytes 288 | tf_op jit(solution)/shard_map/all_to_all | solution.py:148
  40.7 50.0 %while.38 = (s32[]{:T(128)}, bf16[1,4,8,4]{2,1,3,0:T(4,128)(2,1)S(1)}, s32[]{:T(128)}, s32[32]{0:T(128)}, s32[32]{0:T(128)}, /*index=5*/f32[1,2,4,8192]{3,2,1,0:...) while((s32[]{:T(128)}, ...), condition=%wide.region_3.5_spmd, body=%wide.region_2.4_spmd.sunk | while | flops 2973951 | bytes 806209 | solution.py:158
  46.5 4.4 %cosine_convert_fusion.2 = (bf16[8,8192]{1,0:T(8,128)(2,1)S(1)}, bf16[8,8192]{1,0:T(8,128)(2,1)S(1)}) fusion(f32[]{:T(128)S(6)} %div.51, s32[]{:T(128)S(6)} %select_n.309, s32[8192]{0:T(1024)S(1)} %multiply_add_fusion.2, s32[8]{0:T(128)} %get-tuple-element.495, pred[]{:T(512)S(6)} %lt.246), kind=kLoop, calls=%fused_computation.24.clone.1 | loop fusion | flops 786432 | bytes 294953 | tf_op jit(solution)/shard_map/convert.5
  56.4 1.2 dynamic_slice.80
  59.0 4.4 %cosine_convert_fusion.2 = (bf16[8,8192]{1,0:T(8,128)(2,1)S(1)}, bf16[8,8192]{1,0:T(8,128)(2,1)S(1)}) fusion(f32[]{:T(128)S(6)} %div.51, s32[]{:T(128)S(6)} %select_n.309, s32[8192]{0:T(1024)S(1)} %multiply_add_fusion.2, s32[8]{0:T(128)} %get-tuple-element.495, pred[]{:T(512)S(6)} %lt.246), kind=kLoop, calls=%fused_computation.24.clone.1 | loop fusion | flops 786432 | bytes 294953 | tf_op jit(solution)/shard_map/convert.5
  68.9 1.2 dynamic_slice.80
  71.5 4.4 %cosine_convert_fusion.2 = (bf16[8,8192]{1,0:T(8,128)(2,1)S(1)}, bf16[8,8192]{1,0:T(8,128)(2,1)S(1)}) fusion(f32[]{:T(128)S(6)} %div.51, s32[]{:T(128)S(6)} %select_n.309, s32[8192]{0:T(1024)S(1)} %multiply_add_fusion.2, s32[8]{0:T(128)} %get-tuple-element.495, pred[]{:T(512)S(6)} %lt.246), kind=kLoop, calls=%fused_computation.24.clone.1 | loop fusion | flops 786432 | bytes 294953 | tf_op jit(solution)/shard_map/convert.5
  84.0 4.4 %cosine_convert_fusion.2 = (bf16[8,8192]{1,0:T(8,128)(2,1)S(1)}, bf16[8,8192]{1,0:T(8,128)(2,1)S(1)}) fusion(f32[]{:T(128)S(6)} %div.51, s32[]{:T(128)S(6)} %select_n.309, s32[8192]{0:T(1024)S(1)} %multiply_add_fusion.2, s32[8]{0:T(128)} %get-tuple-element.495, pred[]{:T(512)S(6)} %lt.246), kind=kLoop, calls=%fused_computation.24.clone.1 | loop fusion | flops 786432 | bytes 294953 | tf_op jit(solution)/shard_map/convert.5
  92.3 4.1 %collective-permute-start.2 = (bf16[1,4,1,4]{2,1,3,0:T(4,128)(2,1)S(1)}, bf16[1,4,1,4]{2,1,3,0:T(4,128)(2,1)S(1)}, u32[]{:S(2)}, u32[]{:S(2)}) collective-permute-start(bf16[1,4,1,4]{2,1,3,0:T(4,128)(2,1)S(1)} %get-tuple-element.294), channel_id=1, source_target_pairs={{0,3},{1,4},{2,5},{3,6},{4,7},{5,0},{6,1},{7,2},{8,11},{9,12},{10,... | collective-permute-start | bytes 104 | tf_op jit(solution)/shard_map/ppermute | solution.py:26
  97.0 2.3 %collective-permute-start.4 = (bf16[1,4,1,4]{2,1,3,0:T(4,128)(2,1)S(1)}, bf16[1,4,1,4]{2,1,3,0:T(4,128)(2,1)S(1)}, u32[]{:S(2)}, u32[]{:S(2)}) collective-permute-start(bf16[1,4,1,4]{2,1,3,0:T(4,128)(2,1)S(1)} %get-tuple-element.292), channel_id=1, source_target_pairs={{0,5},{1,6},{2,7},{3,0},{4,1},{5,2},{6,3},{7,4},{8,13},{9,14},{10,... | collective-permute-start | bytes 104 | tf_op jit(solution)/shard_map/ppermute | solution.py:26
  99.4 2.4 %collective-permute-start.6 = (bf16[1,4,1,4]{2,1,3,0:T(4,128)(2,1)S(1)}, bf16[1,4,1,4]{2,1,3,0:T(4,128)(2,1)S(1)}, u32[]{:S(2)}, u32[]{:S(2)}) collective-permute-start(bf16[1,4,1,4]{2,1,3,0:T(4,128)(2,1)S(1)} %get-tuple-element.290), channel_id=1, source_target_pairs={{0,7},{1,0},{2,1},{3,2},{4,3},{5,4},{6,5},{7,6},{8,15},{9,8},{10,9... | collective-permute-start | bytes 104 | tf_op jit(solution)/shard_map/ppermute | solution.py:26
  105.7 8.8 %while.39 = (s32[]{:T(128)}, f32[4,4096]{1,0:T(4,128)S(1)}, bf16[2,1,4096,32]{2,3,1,0:T(8,128)(2,1)}, bf16[4,32]{1,0:T(4,128)(2,1)S(1)}, bf16[4,32]{1,0:T(4,128)...) while((s32[]{:T(128)}, f32[4,4096]{1,0:T(4,128)S(1)}, ...), condition=%wide.region_6.8_spmd, body=%wide.region_5.7_spmd.sunk | while | flops 264199 | bytes 93091 | solution.py:183
  114.6 2.0 %copy.72 = f32[4,4096]{0,1:T(8,128)} copy(f32[4,4096]{1,0:T(4,128)S(1)} %get-tuple-element.203) | data formatting | bytes 131072 | tf_op jit(solution)/shard_map/while | solution.py:183
  116.5 2.2 %broadcast_multiply_fusion = f32[4,4096]{0,1:T(8,128)S(1)} fusion(f32[4,4096]{0,1:T(8,128)} %copy.72, f32[4096]{0:T(1024)S(1)} %fusion.44), kind=kLoop, calls=%fused_computation.59 | loop fusion | flops 16384 | bytes 147456 | tf_op jit(solution)/shard_map/mul | solution.py:187
  119.3 19.4 %reduce = f32[4096,4]{1,0:T(8,128)} reduce(f32[4096,1,1,4]{3,2,1,0:T(1,128)S(1)} %bitcast.141, f32[]{:T(128)} %broadcast.309), dimensions={1,2}, to_apply=%bitcast.103.reduce_sub_computation | reduce | bytes 131076
  138.6 3.9 %reshape.454 = f32[4,1,4096]{2,1,0:T(1,128)} reshape(f32[4096,4]{1,0:T(8,128)} %reduce) | data formatting | bytes 131072
  142.5 3.5 %all-to-all-start.1 = ((f32[4,1,4096]{2,1,0:T(1,128)}), f32[4,1,4096]{2,1,0:T(1,128)S(1)}, u32[]{:S(2)}, u32[]{:S(2)}) async-start(f32[4,1,4096]{2,1,0:T(1,128)} %reshape.454), calls=%async_computation.1 | async-start | bytes 131072 | tf_op jit(solution)/shard_map/all_to_all | solution.py:188
  146.6 3.3 %all-to-all-done.1 = f32[4,1,4096]{2,1,0:T(1,128)S(1)} async-done(((f32[4,1,4096]{2,1,0:T(1,128)}), f32[4,1,4096]{2,1,0:T(1,128)S(1)}, u32[]{:S(2)}, u32[]{:S(2)}) %all-to-all-start.1) | async-done | bytes 65568 | tf_op jit(solution)/shard_map/all_to_all | solution.py:188
  150.7 3.3 %reshape.455 = f32[4096,1,1,4]{3,2,1,0:T(1,128)S(1)} reshape(f32[4,4096]{1,0:T(4,128)S(1)} %reduce.1) | data formatting | bytes 131072
  (156 shorter events, 55.2 us)
Async XLA Ops:
  30.3 10.4 %all-to-all-start = ((bf16[1,4,1,32]{1,2,0,3:T(2,128)(2,1)}), bf16[1,4,1,32]{1,2,0,3:T(2,128)(2,1)S(1)}, u32[]{:S(2)}, u32[]{:S(2)}) async-start(bf16[1,4,1,32]{1,2,0,3:T(2,128)(2,1)} %copy.54), calls=%async_computation | async-start | bytes 32768 | tf_op jit(solution)/shard_map/all_to_all | solution.py:148
  90.8 8.5 %collective-permute-start = (bf16[1,4,1,4]{2,1,3,0:T(4,128)(2,1)S(1)}, bf16[1,4,1,4]{2,1,3,0:T(4,128)(2,1)S(1)}, u32[]{:S(2)}, u32[]{:S(2)}) collective-permute-start(bf16[1,4,1,4]{2,1,3,0:T(4,128)(2,1)S(1)} %get-tuple-element.296), channel_id=1, source_target_pairs={{0,1},{1,2},{2,3},{3,4},{4,5},{5,6},{6,7},{7,0},{8,9},{9,10},{10,1... | collective-permute-start | bytes 104 | tf_op jit(solution)/shard_map/ppermute | solution.py:26
  91.7 7.8 %collective-permute-start.1 = (bf16[1,4,1,4]{2,1,3,0:T(4,128)(2,1)S(1)}, bf16[1,4,1,4]{2,1,3,0:T(4,128)(2,1)S(1)}, u32[]{:S(2)}, u32[]{:S(2)}) collective-permute-start(bf16[1,4,1,4]{2,1,3,0:T(4,128)(2,1)S(1)} %get-tuple-element.295), channel_id=1, source_target_pairs={{0,2},{1,3},{2,4},{3,5},{4,6},{5,7},{6,0},{7,1},{8,10},{9,11},{10,... | collective-permute-start | bytes 104 | tf_op jit(solution)/shard_map/ppermute | solution.py:26
  92.3 9.7 %collective-permute-start.2 = (bf16[1,4,1,4]{2,1,3,0:T(4,128)(2,1)S(1)}, bf16[1,4,1,4]{2,1,3,0:T(4,128)(2,1)S(1)}, u32[]{:S(2)}, u32[]{:S(2)}) collective-permute-start(bf16[1,4,1,4]{2,1,3,0:T(4,128)(2,1)S(1)} %get-tuple-element.294), channel_id=1, source_target_pairs={{0,3},{1,4},{2,5},{3,6},{4,7},{5,0},{6,1},{7,2},{8,11},{9,12},{10,... | collective-permute-start | bytes 104 | tf_op jit(solution)/shard_map/ppermute | solution.py:26
  96.4 5.7 %collective-permute-start.3 = (bf16[1,4,1,4]{2,1,3,0:T(4,128)(2,1)S(1)}, bf16[1,4,1,4]{2,1,3,0:T(4,128)(2,1)S(1)}, u32[]{:S(2)}, u32[]{:S(2)}) collective-permute-start(bf16[1,4,1,4]{2,1,3,0:T(4,128)(2,1)S(1)} %get-tuple-element.293), channel_id=1, source_target_pairs={{0,4},{1,5},{2,6},{3,7},{4,0},{5,1},{6,2},{7,3},{8,12},{9,13},{10,... | collective-permute-start | bytes 104 | tf_op jit(solution)/shard_map/ppermute | solution.py:26
  97.0 5.3 %collective-permute-start.4 = (bf16[1,4,1,4]{2,1,3,0:T(4,128)(2,1)S(1)}, bf16[1,4,1,4]{2,1,3,0:T(4,128)(2,1)S(1)}, u32[]{:S(2)}, u32[]{:S(2)}) collective-permute-start(bf16[1,4,1,4]{2,1,3,0:T(4,128)(2,1)S(1)} %get-tuple-element.292), channel_id=1, source_target_pairs={{0,5},{1,6},{2,7},{3,0},{4,1},{5,2},{6,3},{7,4},{8,13},{9,14},{10,... | collective-permute-start | bytes 104 | tf_op jit(solution)/shard_map/ppermute | solution.py:26
  99.3 3.6 %collective-permute-start.5 = (bf16[1,4,1,4]{2,1,3,0:T(4,128)(2,1)S(1)}, bf16[1,4,1,4]{2,1,3,0:T(4,128)(2,1)S(1)}, u32[]{:S(2)}, u32[]{:S(2)}) collective-permute-start(bf16[1,4,1,4]{2,1,3,0:T(4,128)(2,1)S(1)} %get-tuple-element.291), channel_id=1, source_target_pairs={{0,6},{1,7},{2,0},{3,1},{4,2},{5,3},{6,4},{7,5},{8,14},{9,15},{10,... | collective-permute-start | bytes 104 | tf_op jit(solution)/shard_map/ppermute | solution.py:26
  99.4 4.6 %collective-permute-start.6 = (bf16[1,4,1,4]{2,1,3,0:T(4,128)(2,1)S(1)}, bf16[1,4,1,4]{2,1,3,0:T(4,128)(2,1)S(1)}, u32[]{:S(2)}, u32[]{:S(2)}) collective-permute-start(bf16[1,4,1,4]{2,1,3,0:T(4,128)(2,1)S(1)} %get-tuple-element.290), channel_id=1, source_target_pairs={{0,7},{1,0},{2,1},{3,2},{4,3},{5,4},{6,5},{7,6},{8,15},{9,8},{10,9... | collective-permute-start | bytes 104 | tf_op jit(solution)/shard_map/ppermute | solution.py:26
  138.6 7.5 %copy-start = (f32[4,3]{1,0:T(4,128)S(1)}, f32[4,3]{1,0:T(4,128)}, u32[]{:S(2)}) copy-start(f32[4,3]{1,0:T(4,128)} %param.21) | copy-start | bytes 148
  142.5 7.4 %all-to-all-start.1 = ((f32[4,1,4096]{2,1,0:T(1,128)}), f32[4,1,4096]{2,1,0:T(1,128)S(1)}, u32[]{:S(2)}, u32[]{:S(2)}) async-start(f32[4,1,4096]{2,1,0:T(1,128)} %reshape.454), calls=%async_computation.1 | async-start | bytes 131072 | tf_op jit(solution)/shard_map/all_to_all | solution.py:188
